TPU v7x, 128 devices: a whole 4x4x4 slice. The times are simulated.
128 devices in a mesh: segment: 2 (over core), seq: 32 (over z_lo, y, x), mp: 2 (over z_hi).
Axes of the slice: x: 4, y: 4, z: 4 (z_hi: 2, z_lo: 2; z = z_hi * 2 + z_lo), core: 2. Of those that a mesh axis runs over, the one named last changes fastest.
Arguments:
- inputs: bfloat16 [65536, 512], P('seq', 'mp'), may hold values from -6 to 6
- cotangent: bfloat16 [65536, 512], P('seq', 'mp'), may hold values from -0.375 to 0.375
- gate_gain: float32 [2, 512], P('segment', 'mp'), may hold values from 0.3 to 3
- key_gain: float32 [2, 512], P('segment', 'mp'), may hold values from 0.3 to 3
- first_factor: bfloat16 [2, 256, 256, 256], P('segment', 'seq'), may hold values from -0.375 to 0.375
- second_factor: bfloat16 [2, 256, 256, 256], P('segment', 'seq'), may hold values from -0.375 to 0.375
- up_first: bfloat16 [2, 4, 128, 128], P('segment', 'mp'), may hold values from -0.5 to 0.5
- up_second: bfloat16 [2, 4, 128, 512], P('segment', 'mp'), may hold values from -0.5 to 0.5
- down_first: bfloat16 [2, 4, 512, 128], P('segment', 'mp'), may hold values from -0.25 to 0.25
- down_second_weight: bfloat16 [2, 4, 128, 128], P('segment', 'mp'), may hold values from -0.5 to 0.5
Outputs:
- grad_first: float32 [2, 256, 256, 256], P('segment', 'seq', 'mp')
- grad_second: float32 [2, 256, 256, 256], P('segment', 'seq', 'mp')
All inputs are finite; a program needn't handle non-finite values.
Results may differ from a plain program's by a relative error of at most 0.024.
Values may be sent and summed in bfloat16 or wider, within the bound.
No kernel may reach another device: no remote copies, remote signals or barrier semaphores. Data moves between devices by JAX's collectives and lax.ppermute only.
A program may use at most 128 MiB of HBM per device.

v0:
```python
import jax
import jax.numpy as jnp
from jax import lax
from jax.sharding import PartitionSpec as P


def shifted(value, axis, steps):
    count = lax.axis_size(axis)
    leading, last = (max(0, -steps), min(count, count - steps))
    return lax.ppermute(value, axis, [(source, source + steps) for source in range(leading, last)])


def sigmoid_slope(values):
    logistic = jax.nn.sigmoid(values)
    return logistic * (1.0 + values * (1.0 - logistic))


def sequence_mix(scaled, first_block, second_block):
    mixed_rows = jnp.einsum(
        "aoi,aic->aoc", first_block, scaled, preferred_element_type=jnp.float32
    ).astype(jnp.bfloat16)
    columns = lax.all_to_all(mixed_rows, "seq", split_axis=1, concat_axis=0, tiled=True)
    turned_cols = jnp.einsum(
        "boi,ibc->obc", second_block, columns, preferred_element_type=jnp.float32
    ).astype(jnp.bfloat16)
    return (lax.all_to_all(turned_cols, "seq", split_axis=0, concat_axis=1, tiled=True), columns)


def sequence_back(back_turned, mixed_cols, second_block):
    back_turned_cols = lax.all_to_all(back_turned, "seq", split_axis=1, concat_axis=0, tiled=True)
    second_grad = jnp.einsum(
        "obc,ibc->boi", back_turned_cols, mixed_cols, preferred_element_type=jnp.float32
    )
    back_mixed_cols = jnp.einsum(
        "boi,obc->ibc", second_block, back_turned_cols, preferred_element_type=jnp.float32
    ).astype(jnp.bfloat16)
    back_mixed = lax.all_to_all(back_mixed_cols, "seq", split_axis=0, concat_axis=1, tiled=True)
    return (back_mixed, second_grad)


def forward_pass(rows_in, weights, with_output):
    (
        gate_gain,
        key_gain,
        first_block,
        second_block,
        up_first,
        up_second,
        down_first,
        down_second_weight,
    ) = weights
    tokens = rows_in.shape[0]
    channels = rows_in.shape[1]
    row_blocks = first_block.shape[0]
    block_size = first_block.shape[1]
    local_blocks = up_first.shape[0]
    block_column_width = up_first.shape[1]
    total_blocks = local_blocks * lax.axis_size("mp")
    sub_width = block_column_width // total_blocks
    rows_grid = rows_in.reshape(row_blocks, block_size, channels).astype(jnp.float32)
    scaled = (rows_grid * key_gain).astype(jnp.bfloat16)
    turned, mixed_cols = sequence_mix(scaled, first_block, second_block)
    gate_pre = rows_grid * gate_gain
    hidden_rows = (rows_grid + jax.nn.silu(gate_pre) * turned.astype(jnp.float32)).astype(
        jnp.bfloat16
    )
    hidden_rows = hidden_rows.reshape(tokens, local_blocks, block_column_width)
    up_grid = up_first.reshape(local_blocks, block_column_width, total_blocks, sub_width)
    permuted = jnp.einsum(
        "tki,kijc->tjkc", hidden_rows, up_grid, preferred_element_type=jnp.float32
    ).astype(jnp.bfloat16)
    permuted = permuted.reshape(tokens, total_blocks, local_blocks * sub_width)
    gathered_in = lax.all_to_all(permuted, "mp", split_axis=1, concat_axis=2, tiled=True)
    preact = jnp.einsum("tjq,jqe->tje", gathered_in, up_second, preferred_element_type=jnp.float32)
    kept_state = (rows_grid, scaled, mixed_cols, turned, preact)
    if not with_output:
        return (None, kept_state)
    active = jax.nn.silu(preact).astype(jnp.bfloat16)
    down_grid = down_first.reshape(local_blocks, down_first.shape[1], total_blocks, sub_width)
    folded_rows = jnp.einsum(
        "tje,jemc->tmjc", active, down_grid, preferred_element_type=jnp.float32
    ).astype(jnp.bfloat16)
    folded_rows = folded_rows.reshape(tokens, total_blocks, local_blocks * sub_width)
    gathered_output = lax.all_to_all(folded_rows, "mp", split_axis=1, concat_axis=2, tiled=True)
    output_portion = jnp.einsum(
        "xds,dsl->xdl", gathered_output, down_second_weight, preferred_element_type=jnp.float32
    )
    result = (
        (hidden_rows.astype(jnp.float32) + output_portion)
        .reshape(tokens, channels)
        .astype(jnp.bfloat16)
    )
    return (result, kept_state)


def backward_pass(cot_rows, kept_state, weights):
    (
        gate_gain,
        key_gain,
        first_block,
        second_block,
        up_first,
        up_second,
        down_first,
        down_second_weight,
    ) = weights
    rows_grid, scaled, mixed_cols, turned, preact = kept_state
    tokens = cot_rows.shape[0]
    channels = cot_rows.shape[1]
    row_blocks = first_block.shape[0]
    block_size = first_block.shape[1]
    local_blocks = up_first.shape[0]
    block_column_width = up_first.shape[1]
    total_blocks = local_blocks * lax.axis_size("mp")
    sub_width = block_column_width // total_blocks
    up_grid = up_first.reshape(local_blocks, block_column_width, total_blocks, sub_width)
    down_grid = down_first.reshape(local_blocks, down_first.shape[1], total_blocks, sub_width)
    backward_folded_rows = jnp.einsum(
        "hsd,sad->hsa",
        cot_rows.reshape(tokens, local_blocks, block_column_width),
        down_second_weight,
        preferred_element_type=jnp.float32,
    ).astype(jnp.bfloat16)
    back_grid = lax.all_to_all(
        backward_folded_rows, "mp", split_axis=2, concat_axis=1, tiled=True
    ).reshape(tokens, total_blocks, local_blocks, sub_width)
    back_active = jnp.einsum(
        "tmjc,jemc->tje", back_grid, down_grid, preferred_element_type=jnp.float32
    )
    back_preact = (back_active * sigmoid_slope(preact)).astype(jnp.bfloat16)
    back_perm = jnp.einsum(
        "tje,jqe->tjq", back_preact, up_second, preferred_element_type=jnp.float32
    ).astype(jnp.bfloat16)
    back_perm_grid = lax.all_to_all(
        back_perm, "mp", split_axis=2, concat_axis=1, tiled=True
    ).reshape(tokens, total_blocks, local_blocks, sub_width)
    back_ffn = jnp.einsum(
        "tjkc,kijc->tki", back_perm_grid, up_grid, preferred_element_type=jnp.float32
    )
    back_hidden = cot_rows.astype(jnp.float32).reshape(
        row_blocks, block_size, channels
    ) + back_ffn.reshape(row_blocks, block_size, channels)
    gate_pre = rows_grid * gate_gain
    back_turned = (back_hidden * jax.nn.silu(gate_pre)).astype(jnp.bfloat16)
    back_mixed, second_grad = sequence_back(back_turned, mixed_cols, second_block)
    first_grad = jnp.einsum("aoc,aic->aoi", back_mixed, scaled, preferred_element_type=jnp.float32)
    back_scaled = jnp.einsum(
        "aoi,aoc->aic", first_block, back_mixed, preferred_element_type=jnp.float32
    )
    back_inputs = (
        back_hidden
        + back_hidden * turned.astype(jnp.float32) * sigmoid_slope(gate_pre) * gate_gain
        + back_scaled * key_gain
    )
    back_inputs = back_inputs.reshape(tokens, channels).astype(jnp.bfloat16)
    return (back_inputs, first_grad, second_grad)


def reduce_channels(first_grad, second_grad):
    totals_first, totals_second = (
        lax.psum(first_grad.astype(jnp.bfloat16), "mp").astype(jnp.float32),
        lax.psum(second_grad.astype(jnp.bfloat16), "mp").astype(jnp.float32),
    )
    half_rows = first_grad.shape[2] // lax.axis_size("mp")
    offset = lax.axis_index("mp") * half_rows
    share_first = lax.dynamic_slice_in_dim(totals_first, offset, half_rows, 2)
    share_second = lax.dynamic_slice_in_dim(totals_second, offset, half_rows, 2)
    return (share_first, share_second)


def on_device(
    inputs,
    cotangent,
    gate_gain,
    key_gain,
    first_factor,
    second_factor,
    up_first,
    up_second,
    down_first,
    down_second_weight,
):
    weights = (
        gate_gain[0],
        key_gain[0],
        first_factor[0],
        second_factor[0],
        up_first[0],
        up_second[0],
        down_first[0],
        down_second_weight[0],
    )
    early_out, early_state = forward_pass(inputs, weights, True)
    received = shifted(early_out, "segment", 1)
    unused_late, later_state = forward_pass(received, weights, False)
    is_first = lax.axis_index("segment") == 0

    def choose_segment(former, latter):
        return jnp.where(is_first, former, latter)

    kept_state = jax.tree.map(choose_segment, early_state, later_state)
    back_upper, first_upper, second_upper = backward_pass(cotangent, kept_state, weights)
    sent_back = shifted(back_upper, "segment", -1)
    back_lower, first_lower, second_lower = backward_pass(sent_back, kept_state, weights)
    first_grad = jnp.where(is_first, first_lower, first_upper)
    second_grad = jnp.where(is_first, second_lower, second_upper)
    return reduce_channels(first_grad[None], second_grad[None])


def solution(mesh):
    placed = (
        P("seq", "mp"),
        P("seq", "mp"),
        P("segment", "mp"),
        P("segment", "mp"),
        P("segment", "seq", None, None),
        P("segment", "seq", None, None),
        P("segment", "mp", None, None),
        P("segment", "mp", None, None),
        P("segment", "mp", None, None),
        P("segment", "mp", None, None),
    )
    return jax.shard_map(
        on_device,
        mesh=mesh,
        in_specs=placed,
        out_specs=(P("segment", "seq", "mp", None), P("segment", "seq", "mp", None)),
        check_vma=False,
    )
```

profile of v0, /device:TPU:1, one launch (start us, length us, event | category | flops | bytes accessed | tf_op | source)
XLA Modules:
  0.0 530.9 jit_solution(14439777909356738681)
XLA Ops:
  11.6 2.6 copy.178
  14.2 24.8 %all_to_all.240 = bf16[8,256,256]{2,0,1:T(8,128)(2,1)S(1)} all-to-all(bf16[8,256,256]{2,0,1:T(8,128)(2,1)} %copy.178), channel_id=1, replica_groups=mesh['segment'=2,'seq'=32,'mp'=2] {'seq'}, dimensions={1} | all-to-all | bytes 2097152 | tf_op jit(solution)/shard_map/all_to_all | solution.py:22
  41.8 2.6 copy.182
  44.5 4.7 all-to-all-start.2
  49.1 2.6 copy.176
  51.8 11.6 %all-to-all-done.2 = bf16[256,8,256]{2,1,0:T(8,128)(2,1)} async-done(((bf16[256,8,256]{2,1,0:T(8,128)(2,1)}), bf16[256,8,256]{2,1,0:T(8,128)(2,1)}, u32[]{:S(2)}, u32[]{:S(2)}) %all-to-all-start.2) | async-done | bytes 1048608 | tf_op jit(solution)/shard_map/all_to_all | solution.py:26
  66.4 3.3 reshape.116
  69.6 4.2 copy.184
  73.8 3.0 add_convert_fusion.1
  77.6 15.9 %all_to_all.241 = bf16[2048,4,64]{0,2,1:T(8,128)(2,1)S(1)} all-to-all(bf16[2048,4,64]{0,2,1:T(8,128)(2,1)S(1)} %bitcast.283), channel_id=1, replica_groups=mesh['segment'=2,'seq'=32,'mp'=2] {'mp'}, dimensions={1} | all-to-all | bytes 2097152 | tf_op jit(solution)/shard_map/all_to_all | solution.py:73
  94.9 2.8 fusion.6
  98.4 13.1 %all_to_all.242 = bf16[2048,4,64]{0,2,1:T(8,128)(2,1)S(1)} all-to-all(bf16[2048,4,64]{0,2,1:T(8,128)(2,1)S(1)} %bitcast.285), channel_id=1, replica_groups=mesh['segment'=2,'seq'=32,'mp'=2] {'mp'}, dimensions={1} | all-to-all | bytes 2097152 | tf_op jit(solution)/shard_map/all_to_all | solution.py:84
  113.4 7.8 %collective-permute-done = bf16[2048,256]{0,1:T(8,128)(2,1)} collective-permute-done((bf16[2048,256]{0,1:T(8,128)(2,1)S(1)}, bf16[2048,256]{0,1:T(8,128)(2,1)}, u32[]{:S(2)}, u32[]{:S(2)}) %collective-permute-start) | collective-permute-done | bytes 1048608 | tf_op jit(solution)/shard_map/ppermute | solution.py:10
  121.2 2.6 copy.194
  123.8 1.9 multiply_convert_fusion.2
  128.2 2.6 copy.196
  130.8 22.3 %all_to_all.243 = bf16[8,256,256]{2,0,1:T(8,128)(2,1)S(1)} all-to-all(bf16[8,256,256]{2,0,1:T(8,128)(2,1)} %copy.196), channel_id=1, replica_groups=mesh['segment'=2,'seq'=32,'mp'=2] {'seq'}, dimensions={1} | all-to-all | bytes 2097152 | tf_op jit(solution)/shard_map/all_to_all | solution.py:22
  155.9 2.6 copy.200
  158.5 4.7 all-to-all-start.6
  164.9 2.1 copy.171
  167.0 2.8 convert_element_type.273
  169.8 8.2 %all-to-all-done.6 = bf16[256,8,256]{2,1,0:T(8,128)(2,1)} async-done(((bf16[256,8,256]{2,1,0:T(8,128)(2,1)}), bf16[256,8,256]{2,1,0:T(8,128)(2,1)}, u32[]{:S(2)}, u32[]{:S(2)}) %all-to-all-start.6) | async-done | bytes 1048608 | tf_op jit(solution)/shard_map/all_to_all | solution.py:26
  177.9 4.4 all-to-all-start
  185.3 3.3 reshape.119
  188.6 4.2 copy.202
  192.8 3.2 fusion.43
  197.2 4.4 all-to-all-start.7
  201.7 1.8 copy.174
  206.1 7.5 %all-to-all-done.7 = bf16[2048,4,64]{0,2,1:T(8,128)(2,1)} async-done(((bf16[2048,4,64]{0,2,1:T(8,128)(2,1)}), bf16[2048,4,64]{0,2,1:T(8,128)(2,1)}, u32[]{:S(2)}, u32[]{:S(2)}) %all-to-all-start.7) | async-done | bytes 1048608 | tf_op jit(solution)/shard_map/all_to_all | solution.py:73
  214.9 7.5 %add_multiply_fusion = f32[2048,2,512]{2,0,1:T(8,128)} fusion(f32[2,2048,512]{2,1,0:T(8,128)} %copy-done.5, bf16[2048,2,128]{0,2,1:T(8,128)(2,1)S(1)} %bitcast.301, pred[]{:T(512)S(6)} %eq.3, bf16[1,2,128,512]{3,2,1,0:T(8,128)(2,1)S(1)} %copy-done.18), kind=kOutput, calls=%fused_computation.10 | convolution fusion | flops 553648128 | bytes 18087936 | tf_op jit(solution)/shard_map/tjq,jqe->tje/dot_general | solution.py:74
  222.4 7.1 %fusion.12 = bf16[2048,2,128]{2,0,1:T(8,128)(2,1)} fusion(f32[2048,2,512]{2,0,1:T(8,128)} %add_multiply_fusion, bf16[2048,4,2,32]{0,3,2,1:T(8,128)(2,1)} %bitcast.298, bf16[1,2,128,512]{3,2,1,0:T(8,128)(2,1)S(1)} %copy-done.18, bf16[2,512,4,32]{1,3,2,0:T(8,128)(2,1)} %bitcast.305), kind=kOutput, calls=%fused_computation.24 | convolution fusion | flops 1078460416 | bytes 11010048 | tf_op jit(solution)/shard_map/tje,jqe->tjq/dot_general | solution.py:131
  229.5 3.7 copy.207
  233.2 4.6 all-to-all-start.8
  238.8 10.1 %all-to-all-done.8 = bf16[2048,2,128]{0,1,2:T(2,128)(2,1)} async-done(((bf16[2048,2,128]{0,1,2:T(2,128)(2,1)}), bf16[2048,2,128]{0,1,2:T(2,128)(2,1)}, u32[]{:S(2)}, u32[]{:S(2)}) %all-to-all-start.8) | async-done | bytes 1048608 | tf_op jit(solution)/shard_map/all_to_all | solution.py:134
  251.0 8.6 %copy.255 = f32[2048,2,128]{2,1,0:T(2,128)} copy(f32[2048,2,128]{2,0,1:T(8,128)S(1)} %convolution_bitcast_fusion.1) | data formatting | bytes 4194304 | tf_op jit(solution)/shard_map/reshape | solution.py:142
  259.6 3.9 reshape.136
  263.5 3.3 multiply_convert_fusion.1
  267.4 20.8 %all_to_all.244 = bf16[8,256,256]{2,0,1:T(8,128)(2,1)S(1)} all-to-all(bf16[8,256,256]{2,0,1:T(8,128)(2,1)S(1)} %copy.214), channel_id=1, replica_groups=mesh['segment'=2,'seq'=32,'mp'=2] {'seq'}, dimensions={1} | all-to-all | bytes 2097152 | tf_op jit(solution)/shard_map/all_to_all | solution.py:30
  291.0 2.6 copy.218
  293.7 5.0 all-to-all-start.10
  298.6 2.3 broadcast_select_fusion.1
  301.0 10.3 %all-to-all-done.10 = bf16[256,8,256]{2,1,0:T(8,128)(2,1)} async-done(((bf16[256,8,256]{2,1,0:T(8,128)(2,1)}), bf16[256,8,256]{2,1,0:T(8,128)(2,1)}, u32[]{:S(2)}, u32[]{:S(2)}) %all-to-all-start.10) | async-done | bytes 1048608 | tf_op jit(solution)/shard_map/all_to_all | solution.py:37
  311.3 6.2 %fusion.14 = bf16[8,256,256]{2,1,0:T(8,128)(2,1)} fusion(f32[8,256,256]{2,1,0:T(8,128)} %reshape.136, bf16[8,256,256]{2,1,0:T(8,128)(2,1)} %bitcast.271, bf16[1,8,256,256]{3,2,1,0:T(8,128)(2,1)} %param.14, f32[256]{0:T(256)S(1)} %bitcast.314, f32[256]{0:T(256)S(1)} %bitcast.310, bf16[8,32,8,256]{3,2,0,1:T(8,128)(2,1)} %bitcast.76, ...), kind=kOutput, calls=%fused_computation.31 | convolution fusion | flops 278396928 | bytes 11536385 | tf_op jit(solution)/shard_map/aoi,aoc->aic/dot_general | solution.py:147
  317.5 2.3 copy.221
  319.7 6.8 %collective-permute-start.1 = (bf16[2048,256]{0,1:T(8,128)(2,1)}, bf16[2048,256]{0,1:T(8,128)(2,1)S(1)}, u32[]{:S(2)}, u32[]{:S(2)}) collective-permute-start(bf16[2048,256]{0,1:T(8,128)(2,1)} %copy.221), channel_id=1, source_target_pairs={{64,0},{65,1},{66,2},{67,3},{68,4},{69,5},{70,6},{71,7},{72,8},{73... | collective-permute-start | bytes 3145736 | tf_op jit(solution)/shard_map/ppermute | solution.py:10
  326.5 2.0 collective-permute-done.1
  331.0 3.7 copy.224
  334.7 18.4 %all_to_all.245 = bf16[2048,2,128]{0,1,2:T(2,128)(2,1)S(1)} all-to-all(bf16[2048,2,128]{0,1,2:T(2,128)(2,1)} %copy.224), channel_id=1, replica_groups=mesh['segment'=2,'seq'=32,'mp'=2] {'mp'}, dimensions={2} | all-to-all | bytes 2097152 | tf_op jit(solution)/shard_map/all_to_all | solution.py:124
  354.5 7.2 %fusion.13 = bf16[2048,2,128]{2,0,1:T(8,128)(2,1)} fusion(f32[2048,2,512]{2,0,1:T(8,128)} %add_multiply_fusion, bf16[2048,4,2,32]{0,3,2,1:T(8,128)(2,1)} %bitcast.300, bf16[1,2,128,512]{3,2,1,0:T(8,128)(2,1)S(1)} %copy-done.18, bf16[2,512,4,32]{1,3,2,0:T(8,128)(2,1)} %bitcast.306), kind=kOutput, calls=%fused_computation.25 | convolution fusion | flops 1078460416 | bytes 11010048 | tf_op jit(solution)/shard_map/tje,jqe->tjq/dot_general | solution.py:131
  361.6 3.7 copy.228
  365.3 4.4 all-to-all-start.12
  369.7 2.6 copy.222
  372.3 11.4 %all-to-all-done.12 = bf16[2048,2,128]{0,1,2:T(2,128)(2,1)} async-done(((bf16[2048,2,128]{0,1,2:T(2,128)(2,1)}), bf16[2048,2,128]{0,1,2:T(2,128)(2,1)}, u32[]{:S(2)}, u32[]{:S(2)}) %all-to-all-start.12) | async-done | bytes 1048608 | tf_op jit(solution)/shard_map/all_to_all | solution.py:134
  386.0 8.6 %copy.232 = f32[2048,2,128]{2,1,0:T(2,128)} copy(f32[2048,2,128]{2,0,1:T(8,128)S(1)} %convolution_bitcast_fusion) | data formatting | bytes 4194304 | tf_op jit(solution)/shard_map/tjkc,kijc->tki/transpose | solution.py:137
  394.6 3.9 reshape.111
  398.4 3.5 multiply_convert_fusion
  402.6 18.7 %all_to_all.246 = bf16[8,256,256]{2,0,1:T(8,128)(2,1)S(1)} all-to-all(bf16[8,256,256]{2,0,1:T(8,128)(2,1)S(1)} %copy.233), channel_id=1, replica_groups=mesh['segment'=2,'seq'=32,'mp'=2] {'seq'}, dimensions={1} | all-to-all | bytes 2097152 | tf_op jit(solution)/shard_map/all_to_all | solution.py:30
  424.1 2.8 copy.237
  426.9 4.9 all-to-all-start.14
  435.9 9.5 %all-to-all-done.14 = bf16[256,8,256]{2,1,0:T(8,128)(2,1)} async-done(((bf16[256,8,256]{2,1,0:T(8,128)(2,1)}), bf16[256,8,256]{2,1,0:T(8,128)(2,1)}, u32[]{:S(2)}, u32[]{:S(2)}) %all-to-all-start.14) | async-done | bytes 1048608 | tf_op jit(solution)/shard_map/all_to_all | solution.py:37
  445.4 1.8 fusion.29
  447.1 2.8 fusion.25
  449.9 71.2 %all-reduce.3.cloned.1.call-done = (bf16[1,8,256,256]{3,2,1,0:T(8,128)(2,1)}, bf16[1,8,256,256]{3,2,1,0:T(8,128)(2,1)}) async-done(((bf16[1,8,256,256]{3,2,1,0:T(8,128)(2,1)}, bf16[1,8,256,256]{3,2,1,0:T(8,128)(2,1)}), (bf16[1,8,256,256]{3,2,1,0:T(8,128)(2,1)}, bf16[1,8,256,256]{3,2,1,0:T(8,128)(2,1)})) %all-reduce.3.cloned.1.call-update) | async-done | bytes 2097168 | tf_op jit(solution)/shard_map/psum | solution.py:161
  521.1 2.7 dynamic-slice_convert_fusion
  (96 shorter events, 49.9 us)
Async XLA Ops:
  7.2 33.2 %copy-start = (bf16[1,8,256,256]{3,2,1,0:T(8,128)(2,1)S(1)}, bf16[1,8,256,256]{3,2,1,0:T(8,128)(2,1)}, u32[]{:S(2)}) copy-start(bf16[1,8,256,256]{3,2,1,0:T(8,128)(2,1)} %param.15) | copy-start | bytes 3145732
  7.2 1.5 copy-start.22
  8.7 1.5 copy-start.6
  8.9 1.0 copy-start.8
  39.4 1.0 copy-start.1
  44.5 18.9 %all-to-all-start.2 = ((bf16[256,8,256]{2,1,0:T(8,128)(2,1)}), bf16[256,8,256]{2,1,0:T(8,128)(2,1)}, u32[]{:S(2)}, u32[]{:S(2)}) async-start(bf16[256,8,256]{2,1,0:T(8,128)(2,1)} %copy.182), calls=%async_computation.2 | async-start | bytes 2097152 | tf_op jit(solution)/shard_map/all_to_all | solution.py:26
  69.6 4.2 copy-start.21
  73.8 3.0 copy-start.19
  77.6 16.0 %copy-start.18 = (bf16[1,2,128,512]{3,2,1,0:T(8,128)(2,1)S(1)}, bf16[1,2,128,512]{3,2,1,0:T(8,128)(2,1)}, u32[]{:S(2)}) copy-start(bf16[1,2,128,512]{3,2,1,0:T(8,128)(2,1)} %param.17) | copy-start | bytes 786436
  93.5 1.3 copy-start.20
  94.9 3.3 copy-start.5
  98.4 13.2 %copy-start.17 = (bf16[1,2,128,128]{3,2,1,0:T(8,128)(2,1)S(1)}, bf16[1,2,128,128]{3,2,1,0:T(8,128)(2,1)}, u32[]{:S(2)}) copy-start(bf16[1,2,128,128]{3,2,1,0:T(8,128)(2,1)} %param.19) | copy-start | bytes 196612
  112.1 9.1 %collective-permute-start = (bf16[2048,256]{0,1:T(8,128)(2,1)S(1)}, bf16[2048,256]{0,1:T(8,128)(2,1)}, u32[]{:S(2)}, u32[]{:S(2)}) collective-permute-start(bf16[2048,256]{0,1:T(8,128)(2,1)S(1)} %bitcast.297), channel_id=1, source_target_pairs={{0,64},{1,65},{2,66},{3,67},{4,68},{5,69},{6,70},{7,71},{8,72},{9,... | collective-permute-start | bytes 3145736 | tf_op jit(solution)/shard_map/ppermute | solution.py:10
  123.8 2.9 copy-start.7
  125.7 1.0 copy-start.10
  153.4 1.0 copy-start.3
  158.5 19.4 %all-to-all-start.6 = ((bf16[256,8,256]{2,1,0:T(8,128)(2,1)}), bf16[256,8,256]{2,1,0:T(8,128)(2,1)}, u32[]{:S(2)}, u32[]{:S(2)}) async-start(bf16[256,8,256]{2,1,0:T(8,128)(2,1)} %copy.200), calls=%async_computation.6 | async-start | bytes 2097152 | tf_op jit(solution)/shard_map/all_to_all | solution.py:26
  177.9 19.3 %all-to-all-start = ((bf16[2048,2,128]{0,1,2:T(2,128)(2,1)}), bf16[2048,2,128]{0,1,2:T(2,128)(2,1)}, u32[]{:S(2)}, u32[]{:S(2)}) async-start(bf16[2048,2,128]{0,1,2:T(2,128)(2,1)} %copy.171), calls=%async_computation | async-start | bytes 2097152 | tf_op jit(solution)/shard_map/all_to_all | solution.py:124
  197.2 16.3 %all-to-all-start.7 = ((bf16[2048,4,64]{0,2,1:T(8,128)(2,1)}), bf16[2048,4,64]{0,2,1:T(8,128)(2,1)}, u32[]{:S(2)}, u32[]{:S(2)}) async-start(bf16[2048,4,64]{0,2,1:T(8,128)(2,1)} %bitcast.281), calls=%async_computation.7 | async-start | bytes 2097152 | tf_op jit(solution)/shard_map/all_to_all | solution.py:73
  233.2 15.7 %all-to-all-start.8 = ((bf16[2048,2,128]{0,1,2:T(2,128)(2,1)}), bf16[2048,2,128]{0,1,2:T(2,128)(2,1)}, u32[]{:S(2)}, u32[]{:S(2)}) async-start(bf16[2048,2,128]{0,1,2:T(2,128)(2,1)} %copy.207), calls=%async_computation.8 | async-start | bytes 2097152 | tf_op jit(solution)/shard_map/all_to_all | solution.py:134
  288.5 1.1 copy-start.12
  293.7 17.6 %all-to-all-start.10 = ((bf16[256,8,256]{2,1,0:T(8,128)(2,1)}), bf16[256,8,256]{2,1,0:T(8,128)(2,1)}, u32[]{:S(2)}, u32[]{:S(2)}) async-start(bf16[256,8,256]{2,1,0:T(8,128)(2,1)} %copy.218), calls=%async_computation.10 | async-start | bytes 2097152 | tf_op jit(solution)/shard_map/all_to_all | solution.py:37
  319.7 8.8 %collective-permute-start.1 = (bf16[2048,256]{0,1:T(8,128)(2,1)}, bf16[2048,256]{0,1:T(8,128)(2,1)S(1)}, u32[]{:S(2)}, u32[]{:S(2)}) collective-permute-start(bf16[2048,256]{0,1:T(8,128)(2,1)} %copy.221), channel_id=1, source_target_pairs={{64,0},{65,1},{66,2},{67,3},{68,4},{69,5},{70,6},{71,7},{72,8},{73... | collective-permute-start | bytes 3145736 | tf_op jit(solution)/shard_map/ppermute | solution.py:10
  328.5 1.0 copy-start.14
  365.3 18.5 %all-to-all-start.12 = ((bf16[2048,2,128]{0,1,2:T(2,128)(2,1)}), bf16[2048,2,128]{0,1,2:T(2,128)(2,1)}, u32[]{:S(2)}, u32[]{:S(2)}) async-start(bf16[2048,2,128]{0,1,2:T(2,128)(2,1)} %copy.228), calls=%async_computation.12 | async-start | bytes 2097152 | tf_op jit(solution)/shard_map/all_to_all | solution.py:134
  421.6 1.0 copy-start.15
  424.1 7.7 %copy-start.2 = (bf16[32,8,8,256]{3,2,1,0:T(8,128)(2,1)S(1)}, bf16[32,8,8,256]{3,2,1,0:T(8,128)(2,1)}, u32[]{:S(2)}) copy-start(bf16[32,8,8,256]{3,2,1,0:T(8,128)(2,1)} %copy-done.1) | copy-start | bytes 3145732
  424.1 7.7 %copy-start.4 = (bf16[32,8,8,256]{3,2,1,0:T(8,128)(2,1)S(1)}, bf16[32,8,8,256]{3,2,1,0:T(8,128)(2,1)}, u32[]{:S(2)}) copy-start(bf16[32,8,8,256]{3,2,1,0:T(8,128)(2,1)} %copy-done.3) | copy-start | bytes 3145732
  426.9 18.5 %all-to-all-start.14 = ((bf16[256,8,256]{2,1,0:T(8,128)(2,1)}), bf16[256,8,256]{2,1,0:T(8,128)(2,1)}, u32[]{:S(2)}, u32[]{:S(2)}) async-start(bf16[256,8,256]{2,1,0:T(8,128)(2,1)} %copy.237), calls=%async_computation.14 | async-start | bytes 2097152 | tf_op jit(solution)/shard_map/all_to_all | solution.py:37
  431.8 89.4 %all-reduce.3.cloned.1.call-start = ((), (), s32[]{:S(2)}) async-start(), calls=%async_computation.15 | async-start | bytes 4194304 | tf_op jit(solution)/shard_map/psum | solution.py:161
  431.8 1.2 copy-start.16
  433.1 1.2 copy-start.13
  434.3 11.1 %copy-start.9 = (bf16[8,256,256]{2,1,0:T(8,128)(2,1)S(1)}, bf16[8,256,256]{2,1,0:T(8,128)(2,1)}, u32[]{:S(2)}) copy-start(bf16[8,256,256]{2,1,0:T(8,128)(2,1)} %copy-done.8) | copy-start | bytes 3145732
  434.3 11.1 %copy-start.11 = (bf16[8,256,256]{2,1,0:T(8,128)(2,1)S(1)}, bf16[8,256,256]{2,1,0:T(8,128)(2,1)}, u32[]{:S(2)}) copy-start(bf16[8,256,256]{2,1,0:T(8,128)(2,1)} %copy-done.10) | copy-start | bytes 3145732
Sparse Core Ops, SparseCore 0:
  450.0 71.0 all-reduce.2
where the time goes:
time: 542 us; the launch traced here: 531 us
  waiting for transfers between devices  150 us (28%)
  blocking collectives  134 us (25%)
  local copies, waits for them, and re-layouts  107 us (20%)
  matrix products  55.9 us (10%)
  starting transfers between devices  45.2 us (8%)
  other arithmetic  24.8 us (5%)
  between operations  14.8 us (3%)
    psum x1, waiting for transfers between devices, reduce_channels(): lax.psum(first_grad.astype(jnp.bfloat16), 'mp').astype(jnp.float32)  71.2 us
    all_to_all x2, blocking collectives, sequence_mix(): lax.all_to_all(mixed_rows, 'seq', split_axis=1, concat_axis=0, tiled=True)  47.1 us
    all_to_all x2, blocking collectives, sequence_back(): lax.all_to_all(back_turned, 'seq', split_axis=1, concat_axis=0, tiled=True)  39.5 us
    all_to_all x2, waiting for transfers between devices, backward_pass(): lax.all_to_all(back_perm, 'mp', split_axis=2, concat_axis=1, tiled=True)  21.5 us
    all_to_all x2, waiting for transfers between devices, sequence_back(): lax.all_to_all(back_mixed_cols, 'seq', split_axis=0, concat_axis=1, tiled...  19.8 us
    all_to_all x2, waiting for transfers between devices, sequence_mix(): lax.all_to_all(turned_cols, 'seq', split_axis=0, concat_axis=1, tiled=True)  19.8 us
    all_to_all x1, blocking collectives, backward_pass(): lax.all_to_all(backward_folded_rows, 'mp', split_axis=2, concat_axis=1, t...  18.4 us
    convert_element_type x6, local copies, waits for them, and re-layouts, forward_pass(): turned.astype(jnp.float32)  17.9 us
  transfers between devices with their start and end apart: 11, of which 10 were waited for; matrix products, arithmetic and copies ran while one was open for 7% of the time, Pallas kernels for 0%

commit v1 on v0

--- a/solution.py
+++ b/solution.py
@@ -4,6 +4,12 @@
 from jax.sharding import PartitionSpec as P
 
 
+def swap_blocks(value, axis, split, join):
+    shards = jnp.split(value, lax.axis_size(axis), axis=split)
+    arrived = lax.all_to_all(jnp.stack(shards), axis, 0, 0)
+    return jnp.concatenate(arrived, axis=join)
+
+
 def shifted(value, axis, steps):
     count = lax.axis_size(axis)
     leading, last = (max(0, -steps), min(count, count - steps))
@@ -23,7 +29,7 @@
     turned_cols = jnp.einsum(
         "boi,ibc->obc", second_block, columns, preferred_element_type=jnp.float32
     ).astype(jnp.bfloat16)
-    return (lax.all_to_all(turned_cols, "seq", split_axis=0, concat_axis=1, tiled=True), columns)
+    return (swap_blocks(turned_cols, "seq", 0, 1), columns)
 
 
 def sequence_back(back_turned, mixed_cols, second_block):

time: 542 us -> 573 us (1.057)
  local copies, waits for them, and re-layouts: 107 us -> 138 us
  blocking collectives: 134 us -> 152 us
  waiting for transfers between devices: 150 us -> 139 us
    unnamed x48 -> x116, local copies, waits for them, and re-layouts: 12.2 us -> 46.9 us
    all_to_all x0 -> x1, blocking collectives: none -> 17.9 us  [sequence_back(): lax.all_to_all(back_mixed_cols, 'seq', split_axis=0, concat_axis=1, tiled...]
    all_to_all x2 -> x1, waiting for transfers between devices: 19.8 us -> 9.94 us  [sequence_back(): lax.all_to_all(back_mixed_cols, 'seq', split_axis=0, concat_axis=1, tiled...]
  transfers between devices with their start and end apart: 11 -> 10, of which waited for: 10 -> 9; matrix products, arithmetic and copies ran while one was open for 7% -> 7% of each run, Pallas kernels for 0% -> 0%
where the time goes in v1:
time: 573 us; the launch traced here: 563 us
  blocking collectives  152 us (27%)
  waiting for transfers between devices  139 us (24%)
  local copies, waits for them, and re-layouts  138 us (24%)
  matrix products  54.4 us (9%)
  starting transfers between devices  40.7 us (7%)
  other arithmetic  24.2 us (4%)
  between operations  14.8 us (3%)
    psum x1, waiting for transfers between devices, reduce_channels(): lax.psum(first_grad.astype(jnp.bfloat16), 'mp').astype(jnp.float32)  70.9 us
    all_to_all x2, blocking collectives, sequence_mix(): lax.all_to_all(mixed_rows, 'seq', split_axis=1, concat_axis=0, tiled=True)  47.1 us
    unnamed x116, local copies, waits for them, and re-layouts  46.9 us
    all_to_all x2, blocking collectives, sequence_back(): lax.all_to_all(back_turned, 'seq', split_axis=1, concat_axis=0, tiled=True)  39.5 us
    all_to_all x2, waiting for transfers between devices, backward_pass(): lax.all_to_all(back_perm, 'mp', split_axis=2, concat_axis=1, tiled=True)  21.2 us
    all_to_all x2, waiting for transfers between devices, swap_blocks(): arrived = lax.all_to_all(jnp.stack(shards), axis, 0, 0)  19.8 us
    convert_element_type x6, local copies, waits for them, and re-layouts, forward_pass(): turned.astype(jnp.float32)  18.9 us
    all_to_all x1, blocking collectives, backward_pass(): lax.all_to_all(backward_folded_rows, 'mp', split_axis=2, concat_axis=1, t...  18.4 us
  transfers between devices with their start and end apart: 10, of which 9 were waited for; matrix products, arithmetic and copies ran while one was open for 7% of the time, Pallas kernels for 0%

profile of v1, /device:TPU:1, one launch (start us, length us, event | category | flops | bytes accessed | tf_op | source)
XLA Modules:
  0.0 562.5 jit_solution(5355308728508289790)
XLA Ops:
  11.6 2.6 copy.159
  14.2 24.8 %all_to_all.232 = bf16[8,256,256]{2,0,1:T(8,128)(2,1)S(1)} all-to-all(bf16[8,256,256]{2,0,1:T(8,128)(2,1)} %copy.159), channel_id=1, replica_groups=mesh['segment'=2,'seq'=32,'mp'=2] {'seq'}, dimensions={1} | all-to-all | bytes 2097152 | tf_op jit(solution)/shard_map/all_to_all | solution.py:28
  59.3 4.7 all-to-all-start.2
  64.0 2.6 copy.157
  66.6 11.6 %all-to-all-done.2 = bf16[32,8,8,256]{3,1,2,0:T(8,128)(2,1)} async-done(((bf16[32,8,8,256]{3,1,2,0:T(8,128)(2,1)}), bf16[32,8,8,256]{3,1,2,0:T(8,128)(2,1)}, u32[]{:S(2)}, u32[]{:S(2)}) %all-to-all-start.2) | async-done | bytes 1048608 | tf_op jit(solution)/shard_map/all_to_all | solution.py:9
  79.7 2.0 copy.162
  81.7 3.3 reshape.112
  84.9 4.2 copy.163
  89.2 3.0 add_convert_fusion.1
  92.9 15.9 %all_to_all.233 = bf16[2048,4,64]{0,2,1:T(8,128)(2,1)S(1)} all-to-all(bf16[2048,4,64]{0,2,1:T(8,128)(2,1)S(1)} %bitcast.534), channel_id=1, replica_groups=mesh['segment'=2,'seq'=32,'mp'=2] {'mp'}, dimensions={1} | all-to-all | bytes 2097152 | tf_op jit(solution)/shard_map/all_to_all | solution.py:79
  110.3 2.8 fusion.6
  113.8 13.1 %all_to_all.234 = bf16[2048,4,64]{0,2,1:T(8,128)(2,1)S(1)} all-to-all(bf16[2048,4,64]{0,2,1:T(8,128)(2,1)S(1)} %bitcast.536), channel_id=1, replica_groups=mesh['segment'=2,'seq'=32,'mp'=2] {'mp'}, dimensions={1} | all-to-all | bytes 2097152 | tf_op jit(solution)/shard_map/all_to_all | solution.py:90
  128.8 7.8 %collective-permute-done = bf16[2048,256]{0,1:T(8,128)(2,1)} collective-permute-done((bf16[2048,256]{0,1:T(8,128)(2,1)S(1)}, bf16[2048,256]{0,1:T(8,128)(2,1)}, u32[]{:S(2)}, u32[]{:S(2)}) %collective-permute-start) | collective-permute-done | bytes 1048608 | tf_op jit(solution)/shard_map/ppermute | solution.py:16
  136.6 2.6 copy.173
  139.2 1.9 multiply_convert_fusion.2
  143.5 2.6 copy.175
  146.2 22.3 %all_to_all.235 = bf16[8,256,256]{2,0,1:T(8,128)(2,1)S(1)} all-to-all(bf16[8,256,256]{2,0,1:T(8,128)(2,1)} %copy.175), channel_id=1, replica_groups=mesh['segment'=2,'seq'=32,'mp'=2] {'seq'}, dimensions={1} | all-to-all | bytes 2097152 | tf_op jit(solution)/shard_map/all_to_all | solution.py:28
  188.7 4.7 all-to-all-start.6
  193.4 1.7 fusion.10
  195.1 2.0 copy.152
  197.1 2.8 convert_element_type.261
  199.9 8.2 %all-to-all-done.6 = bf16[32,8,8,256]{3,1,2,0:T(8,128)(2,1)} async-done(((bf16[32,8,8,256]{3,1,2,0:T(8,128)(2,1)}), bf16[32,8,8,256]{3,1,2,0:T(8,128)(2,1)}, u32[]{:S(2)}, u32[]{:S(2)}) %all-to-all-start.6) | async-done | bytes 1048608 | tf_op jit(solution)/shard_map/all_to_all | solution.py:9
  208.1 4.4 all-to-all-start
  212.6 3.5 convert_bitcast_fusion
  216.1 1.9 copy.178
  218.0 3.3 reshape.115
  221.3 4.1 copy.179
  225.4 3.2 fusion.43
  229.8 4.4 all-to-all-start.7
  234.3 1.8 copy.155
  238.7 7.2 %all-to-all-done.7 = bf16[2048,4,64]{0,2,1:T(8,128)(2,1)} async-done(((bf16[2048,4,64]{0,2,1:T(8,128)(2,1)}), bf16[2048,4,64]{0,2,1:T(8,128)(2,1)}, u32[]{:S(2)}, u32[]{:S(2)}) %all-to-all-start.7) | async-done | bytes 1048608 | tf_op jit(solution)/shard_map/all_to_all | solution.py:79
  247.2 7.5 %add_multiply_fusion = f32[2048,2,512]{2,0,1:T(8,128)} fusion(f32[2,2048,512]{2,1,0:T(8,128)} %copy-done.2, bf16[2048,2,128]{0,2,1:T(8,128)(2,1)S(1)} %bitcast.553, pred[]{:T(512)S(6)} %eq.3, bf16[1,2,128,512]{3,2,1,0:T(8,128)(2,1)S(1)} %copy-done.21), kind=kOutput, calls=%fused_computation.10 | convolution fusion | flops 553648128 | bytes 18087936 | tf_op jit(solution)/shard_map/tjq,jqe->tje/dot_general | solution.py:80
  254.7 7.1 %fusion.12 = bf16[2048,2,128]{2,0,1:T(8,128)(2,1)} fusion(f32[2048,2,512]{2,0,1:T(8,128)} %add_multiply_fusion, bf16[2048,4,2,32]{0,3,2,1:T(8,128)(2,1)} %bitcast.551, bf16[1,2,128,512]{3,2,1,0:T(8,128)(2,1)S(1)} %copy-done.21, bf16[2,512,4,32]{1,3,2,0:T(8,128)(2,1)} %bitcast.557), kind=kOutput, calls=%fused_computation.24 | convolution fusion | flops 1078460416 | bytes 11010048 | tf_op jit(solution)/shard_map/tje,jqe->tjq/dot_general | solution.py:137
  261.8 3.7 copy.184
  265.5 4.6 all-to-all-start.8
  271.1 9.8 %all-to-all-done.8 = bf16[2048,2,128]{0,1,2:T(2,128)(2,1)} async-done(((bf16[2048,2,128]{0,1,2:T(2,128)(2,1)}), bf16[2048,2,128]{0,1,2:T(2,128)(2,1)}, u32[]{:S(2)}, u32[]{:S(2)}) %all-to-all-start.8) | async-done | bytes 1048608 | tf_op jit(solution)/shard_map/all_to_all | solution.py:140
  283.1 8.6 %copy.230 = f32[2048,2,128]{2,1,0:T(2,128)} copy(f32[2048,2,128]{2,0,1:T(8,128)S(1)} %convolution_bitcast_fusion.1) | data formatting | bytes 4194304 | tf_op jit(solution)/shard_map/reshape | solution.py:148
  291.6 3.9 reshape.129
  295.5 3.3 multiply_convert_fusion.1
  299.4 20.8 %all_to_all.236 = bf16[8,256,256]{2,0,1:T(8,128)(2,1)S(1)} all-to-all(bf16[8,256,256]{2,0,1:T(8,128)(2,1)S(1)} %copy.191), channel_id=1, replica_groups=mesh['segment'=2,'seq'=32,'mp'=2] {'seq'}, dimensions={1} | all-to-all | bytes 2097152 | tf_op jit(solution)/shard_map/all_to_all | solution.py:36
  323.0 2.6 copy.195
  325.7 17.9 %all_to_all.237 = bf16[256,8,256]{2,1,0:T(8,128)(2,1)S(1)} all-to-all(bf16[256,8,256]{2,1,0:T(8,128)(2,1)} %copy.195), channel_id=1, replica_groups=mesh['segment'=2,'seq'=32,'mp'=2] {'seq'}, dimensions={0} | all-to-all | bytes 2097152 | tf_op jit(solution)/shard_map/all_to_all | solution.py:43
  343.6 6.1 %fusion.14 = bf16[8,256,256]{2,1,0:T(8,128)(2,1)} fusion(f32[8,256,256]{2,0,1:T(8,128)} %bitcast.544, f32[8,256,256]{2,1,0:T(8,128)} %reshape.129, bf16[8,256,256]{2,1,0:T(8,128)(2,1)} %bitcast.517, bf16[1,8,256,256]{3,2,1,0:T(8,128)(2,1)} %param.14, f32[256]{0:T(256)S(1)} %bitcast.566, f32[256]{0:T(256)S(1)} %bitcast.562, ...), kind=kOutput, calls=%fused_computation.28 | convolution fusion | flops 277872640 | bytes 12584961 | tf_op jit(solution)/shard_map/aoi,aoc->aic/dot_general | solution.py:153
  349.7 2.3 copy.198
  351.9 7.2 %collective-permute-start.1 = (bf16[2048,256]{0,1:T(8,128)(2,1)}, bf16[2048,256]{0,1:T(8,128)(2,1)S(1)}, u32[]{:S(2)}, u32[]{:S(2)}) collective-permute-start(bf16[2048,256]{0,1:T(8,128)(2,1)} %copy.198), channel_id=1, source_target_pairs={{64,0},{65,1},{66,2},{67,3},{68,4},{69,5},{70,6},{71,7},{72,8},{73... | collective-permute-start | bytes 3145736 | tf_op jit(solution)/shard_map/ppermute | solution.py:16
  359.2 2.0 collective-permute-done.1
  363.7 3.7 copy.201
  367.4 18.4 %all_to_all.238 = bf16[2048,2,128]{0,1,2:T(2,128)(2,1)S(1)} all-to-all(bf16[2048,2,128]{0,1,2:T(2,128)(2,1)} %copy.201), channel_id=1, replica_groups=mesh['segment'=2,'seq'=32,'mp'=2] {'mp'}, dimensions={2} | all-to-all | bytes 2097152 | tf_op jit(solution)/shard_map/all_to_all | solution.py:130
  387.2 7.1 %fusion.13 = bf16[2048,2,128]{2,0,1:T(8,128)(2,1)} fusion(f32[2048,2,512]{2,0,1:T(8,128)} %add_multiply_fusion, bf16[2048,4,2,32]{0,3,2,1:T(8,128)(2,1)} %bitcast.552, bf16[1,2,128,512]{3,2,1,0:T(8,128)(2,1)S(1)} %copy-done.21, bf16[2,512,4,32]{1,3,2,0:T(8,128)(2,1)} %bitcast.558), kind=kOutput, calls=%fused_computation.25 | convolution fusion | flops 1078460416 | bytes 11010048 | tf_op jit(solution)/shard_map/tje,jqe->tjq/dot_general | solution.py:137
  394.3 3.7 copy.205
  398.0 4.4 all-to-all-start.12
  402.4 2.6 copy.199
  405.0 11.5 %all-to-all-done.12 = bf16[2048,2,128]{0,1,2:T(2,128)(2,1)} async-done(((bf16[2048,2,128]{0,1,2:T(2,128)(2,1)}), bf16[2048,2,128]{0,1,2:T(2,128)(2,1)}, u32[]{:S(2)}, u32[]{:S(2)}) %all-to-all-start.12) | async-done | bytes 1048608 | tf_op jit(solution)/shard_map/all_to_all | solution.py:140
  418.7 8.6 %copy.209 = f32[2048,2,128]{2,1,0:T(2,128)} copy(f32[2048,2,128]{2,0,1:T(8,128)S(1)} %convolution_bitcast_fusion) | data formatting | bytes 4194304 | tf_op jit(solution)/shard_map/tjkc,kijc->tki/transpose | solution.py:143
  427.2 3.9 reshape.107
  431.1 3.5 multiply_convert_fusion
  435.2 18.7 %all_to_all.239 = bf16[8,256,256]{2,0,1:T(8,128)(2,1)S(1)} all-to-all(bf16[8,256,256]{2,0,1:T(8,128)(2,1)S(1)} %copy.210), channel_id=1, replica_groups=mesh['segment'=2,'seq'=32,'mp'=2] {'seq'}, dimensions={1} | all-to-all | bytes 2097152 | tf_op jit(solution)/shard_map/all_to_all | solution.py:36
  456.7 2.8 copy.214
  459.5 4.9 all-to-all-start.14
  464.5 1.9 fusion.49
  468.1 9.9 %all-to-all-done.14 = bf16[256,8,256]{2,1,0:T(8,128)(2,1)} async-done(((bf16[256,8,256]{2,1,0:T(8,128)(2,1)}), bf16[256,8,256]{2,1,0:T(8,128)(2,1)}, u32[]{:S(2)}, u32[]{:S(2)}) %all-to-all-start.14) | async-done | bytes 1048608 | tf_op jit(solution)/shard_map/all_to_all | solution.py:43
  478.0 2.2 fusion.29
  481.8 70.9 %all-reduce.3.cloned.1.call-done = (bf16[1,8,256,256]{3,2,1,0:T(8,128)(2,1)}, bf16[1,8,256,256]{3,2,1,0:T(8,128)(2,1)}) async-done(((bf16[1,8,256,256]{3,2,1,0:T(8,128)(2,1)}, bf16[1,8,256,256]{3,2,1,0:T(8,128)(2,1)}), (bf16[1,8,256,256]{3,2,1,0:T(8,128)(2,1)}, bf16[1,8,256,256]{3,2,1,0:T(8,128)(2,1)})) %all-reduce.3.cloned.1.call-update) | async-done | bytes 2097168 | tf_op jit(solution)/shard_map/psum | solution.py:167
  552.8 2.7 dynamic-slice_convert_fusion
  (159 shorter events, 77.8 us)
Async XLA Ops:
  7.2 31.9 %copy-start = (bf16[1,8,256,256]{3,2,1,0:T(8,128)(2,1)S(1)}, bf16[1,8,256,256]{3,2,1,0:T(8,128)(2,1)}, u32[]{:S(2)}) copy-start(bf16[1,8,256,256]{3,2,1,0:T(8,128)(2,1)} %param.15) | copy-start | bytes 3145732
  7.2 1.5 copy-start.25
  8.7 1.5 copy-start.3
  8.9 1.0 copy-start.5
  39.0 10.4 %copy-start.7 = (bf16[8,256,256]{2,0,1:T(8,128)(2,1)}, bf16[8,256,256]{2,0,1:T(8,128)(2,1)S(1)}, u32[]{:S(2)}) copy-start(bf16[8,256,256]{2,0,1:T(8,128)(2,1)S(1)} %all_to_all.232) | copy-start | bytes 3145732
  59.3 18.9 %all-to-all-start.2 = ((bf16[32,8,8,256]{3,1,2,0:T(8,128)(2,1)}), bf16[32,8,8,256]{3,1,2,0:T(8,128)(2,1)}, u32[]{:S(2)}, u32[]{:S(2)}) async-start(bf16[32,8,8,256]{3,1,2,0:T(8,128)(2,1)} %constant_dynamic-update-slice_fusion), calls=%async_computation.2 | async-start | bytes 2097152 | tf_op jit(solution)/shard_map/all_to_all | solution.py:9
  84.9 4.2 copy-start.24
  89.2 3.0 copy-start.22
  92.9 16.0 %copy-start.21 = (bf16[1,2,128,512]{3,2,1,0:T(8,128)(2,1)S(1)}, bf16[1,2,128,512]{3,2,1,0:T(8,128)(2,1)}, u32[]{:S(2)}) copy-start(bf16[1,2,128,512]{3,2,1,0:T(8,128)(2,1)} %param.17) | copy-start | bytes 786436
  108.9 1.3 copy-start.23
  110.2 3.3 copy-start.2
  113.8 13.2 %copy-start.20 = (bf16[1,2,128,128]{3,2,1,0:T(8,128)(2,1)S(1)}, bf16[1,2,128,128]{3,2,1,0:T(8,128)(2,1)}, u32[]{:S(2)}) copy-start(bf16[1,2,128,128]{3,2,1,0:T(8,128)(2,1)} %param.19) | copy-start | bytes 196612
  127.5 9.1 %collective-permute-start = (bf16[2048,256]{0,1:T(8,128)(2,1)S(1)}, bf16[2048,256]{0,1:T(8,128)(2,1)}, u32[]{:S(2)}, u32[]{:S(2)}) collective-permute-start(bf16[2048,256]{0,1:T(8,128)(2,1)S(1)} %bitcast.548), channel_id=1, source_target_pairs={{0,64},{1,65},{2,66},{3,67},{4,68},{5,69},{6,70},{7,71},{8,72},{9,... | collective-permute-start | bytes 3145736 | tf_op jit(solution)/shard_map/ppermute | solution.py:16
  139.2 2.8 copy-start.4
  141.1 1.0 copy-start.9
  168.4 10.4 %copy-start.11 = (bf16[8,256,256]{2,0,1:T(8,128)(2,1)}, bf16[8,256,256]{2,0,1:T(8,128)(2,1)S(1)}, u32[]{:S(2)}) copy-start(bf16[8,256,256]{2,0,1:T(8,128)(2,1)S(1)} %all_to_all.235) | copy-start | bytes 3145732
  188.7 19.4 %all-to-all-start.6 = ((bf16[32,8,8,256]{3,1,2,0:T(8,128)(2,1)}), bf16[32,8,8,256]{3,1,2,0:T(8,128)(2,1)}, u32[]{:S(2)}, u32[]{:S(2)}) async-start(bf16[32,8,8,256]{3,1,2,0:T(8,128)(2,1)} %constant_dynamic-update-slice_fusion.32), calls=%async_computation.6 | async-start | bytes 2097152 | tf_op jit(solution)/shard_map/all_to_all | solution.py:9
  208.1 21.7 %all-to-all-start = ((bf16[2048,2,128]{0,1,2:T(2,128)(2,1)}), bf16[2048,2,128]{0,1,2:T(2,128)(2,1)}, u32[]{:S(2)}, u32[]{:S(2)}) async-start(bf16[2048,2,128]{0,1,2:T(2,128)(2,1)} %copy.152), calls=%async_computation | async-start | bytes 2097152 | tf_op jit(solution)/shard_map/all_to_all | solution.py:130
  229.8 16.0 %all-to-all-start.7 = ((bf16[2048,4,64]{0,2,1:T(8,128)(2,1)}), bf16[2048,4,64]{0,2,1:T(8,128)(2,1)}, u32[]{:S(2)}, u32[]{:S(2)}) async-start(bf16[2048,4,64]{0,2,1:T(8,128)(2,1)} %bitcast.533), calls=%async_computation.7 | async-start | bytes 2097152 | tf_op jit(solution)/shard_map/all_to_all | solution.py:79
  265.5 15.4 %all-to-all-start.8 = ((bf16[2048,2,128]{0,1,2:T(2,128)(2,1)}), bf16[2048,2,128]{0,1,2:T(2,128)(2,1)}, u32[]{:S(2)}, u32[]{:S(2)}) async-start(bf16[2048,2,128]{0,1,2:T(2,128)(2,1)} %copy.184), calls=%async_computation.8 | async-start | bytes 2097152 | tf_op jit(solution)/shard_map/all_to_all | solution.py:140
  320.5 1.0 copy-start.14
  325.7 17.9 %copy-start.1 = (f32[2048,256]{1,0:T(8,128)S(1)}, f32[2048,256]{1,0:T(8,128)}, u32[]{:S(2)}) copy-start(f32[2048,256]{1,0:T(8,128)} %copy.173) | copy-start | bytes 6291460
  343.6 6.1 %copy-start.18 = (bf16[256,8,256]{2,1,0:T(8,128)(2,1)}, bf16[256,8,256]{2,1,0:T(8,128)(2,1)S(1)}, u32[]{:S(2)}) copy-start(bf16[256,8,256]{2,1,0:T(8,128)(2,1)S(1)} %all_to_all.237) | copy-start | bytes 3145732
  351.9 9.2 %collective-permute-start.1 = (bf16[2048,256]{0,1:T(8,128)(2,1)}, bf16[2048,256]{0,1:T(8,128)(2,1)S(1)}, u32[]{:S(2)}, u32[]{:S(2)}) collective-permute-start(bf16[2048,256]{0,1:T(8,128)(2,1)} %copy.198), channel_id=1, source_target_pairs={{64,0},{65,1},{66,2},{67,3},{68,4},{69,5},{70,6},{71,7},{72,8},{73... | collective-permute-start | bytes 3145736 | tf_op jit(solution)/shard_map/ppermute | solution.py:16
  361.2 1.0 copy-start.16
  398.0 18.5 %all-to-all-start.12 = ((bf16[2048,2,128]{0,1,2:T(2,128)(2,1)}), bf16[2048,2,128]{0,1,2:T(2,128)(2,1)}, u32[]{:S(2)}, u32[]{:S(2)}) async-start(bf16[2048,2,128]{0,1,2:T(2,128)(2,1)} %copy.205), calls=%async_computation.12 | async-start | bytes 2097152 | tf_op jit(solution)/shard_map/all_to_all | solution.py:140
  454.3 1.0 copy-start.17
  456.7 7.7 %copy-start.8 = (bf16[8,256,256]{2,0,1:T(8,128)(2,1)S(1)}, bf16[8,256,256]{2,0,1:T(8,128)(2,1)}, u32[]{:S(2)}) copy-start(bf16[8,256,256]{2,0,1:T(8,128)(2,1)} %copy-done.7) | copy-start | bytes 3145732
  456.7 7.7 %copy-start.12 = (bf16[8,256,256]{2,0,1:T(8,128)(2,1)S(1)}, bf16[8,256,256]{2,0,1:T(8,128)(2,1)}, u32[]{:S(2)}) copy-start(bf16[8,256,256]{2,0,1:T(8,128)(2,1)} %copy-done.11) | copy-start | bytes 3145732
  459.5 18.5 %all-to-all-start.14 = ((bf16[256,8,256]{2,1,0:T(8,128)(2,1)}), bf16[256,8,256]{2,1,0:T(8,128)(2,1)}, u32[]{:S(2)}, u32[]{:S(2)}) async-start(bf16[256,8,256]{2,1,0:T(8,128)(2,1)} %copy.214), calls=%async_computation.14 | async-start | bytes 2097152 | tf_op jit(solution)/shard_map/all_to_all | solution.py:43
  464.4 88.3 %all-reduce.3.cloned.1.call-start = ((), (), s32[]{:S(2)}) async-start(), calls=%async_computation.15 | async-start | bytes 4194304 | tf_op jit(solution)/shard_map/psum | solution.py:167
  464.5 2.0 copy-start.13
  464.5 2.0 copy-start.15
  466.5 11.6 %copy-start.6 = (bf16[8,256,256]{2,1,0:T(8,128)(2,1)S(1)}, bf16[8,256,256]{2,1,0:T(8,128)(2,1)}, u32[]{:S(2)}) copy-start(bf16[8,256,256]{2,1,0:T(8,128)(2,1)} %copy-done.5) | copy-start | bytes 3145732
  478.0 2.2 copy-start.10
  478.0 2.2 copy-start.19
Sparse Core Ops, SparseCore 0:
  482.0 70.7 all-reduce.2
